TPU v7x, 32 devices: a whole 2x2x4 slice. The times are simulated.
32 devices in a mesh: slc: 16 (over z, y, core), col: 2 (over x).
Axes of the slice: x: 2, y: 2, z: 4, core: 2. Of those that a mesh axis runs over, the one named last changes fastest.
Arguments:
- basis: bfloat16 [16, 2, 1152, 3456], P('slc', None, None, 'col'), may hold values from -6 to 6
- picks: int32 [16, 608], P('slc', 'col'), may hold values from 0 to 1727, as said below
- coil_maps: bfloat16 [128, 16, 2, 32, 128], P('slc'), may hold values from -6 to 6
Outputs:
- mapped: bfloat16 [128, 16, 2, 32, 128], P('slc', None, None, 'col')
Inputs may be any that keep to these rules, and one draw needn't show every extreme that they name: `picks`: for each slice, the entries in each of the 2 blocks of 304 positions are distinct offsets within the corresponding block of 1728 calibration windows.
All inputs are finite; a program needn't handle non-finite values.
Results may differ from a plain program's by a relative error of at most 0.0049.
Values may be sent and summed in bfloat16 or wider, within the bound.
A program may use at most 448 MiB of HBM per device.

v0:
```python
import math

import jax
import jax.numpy as jnp
from jax import lax
from jax.sharding import PartitionSpec as P

COILS = 32
KSIZE = 6
RANK = 608
IMG = 128


def phase_tables(span, length):
    centre = (span - 1) // 2
    offsets = jnp.arange(span) - centre
    columns = jnp.arange(length)
    turns = offsets[:, None] * columns[None, :] % length
    angles = turns.astype(jnp.float32) * (2.0 * math.pi / length)
    return (jnp.cos(angles), jnp.sin(angles))


def shift_table(count):
    first = jnp.arange(count)[:, None, None]
    second = jnp.arange(count)[None, :, None]
    target = jnp.arange(2 * count - 1)[None, None, :]
    return (second - first + count - 1 == target).astype(jnp.float32)


def outer_gram(left_rows, right_rows):

    def product(left_op, right_op):
        return jnp.einsum("sak,sbk->sab", left_op, right_op, preferred_element_type=jnp.float32)

    real_part = product(left_rows[:, 0], right_rows[:, 0]) + product(
        left_rows[:, 1], right_rows[:, 1]
    )
    imag_part = product(left_rows[:, 1], right_rows[:, 0]) - product(
        left_rows[:, 0], right_rows[:, 1]
    )
    return jnp.stack([real_part, imag_part], axis=1)


def kernel_sums(gram):
    coil_rows = gram.shape[2] // (KSIZE * KSIZE)
    blocks = gram.reshape(gram.shape[0], 2, coil_rows, KSIZE, KSIZE, COILS, KSIZE, KSIZE)
    shifts = shift_table(KSIZE)
    return jnp.einsum(
        "srcaxdby,abp,xyq->srcdpq", blocks, shifts, shifts, precision=lax.Precision.HIGHEST
    )


def column_transform(kernels, cos_table, sin_table, factor):

    def apply_table(values_in, table):
        return jnp.einsum("scdpq,qy->sycdp", values_in, table, precision=lax.Precision.HIGHEST)

    real_part = apply_table(kernels[:, 0], cos_table) - apply_table(kernels[:, 1], sin_table)
    imag_part = apply_table(kernels[:, 0], sin_table) + apply_table(kernels[:, 1], cos_table)
    stacked = jnp.stack([real_part, imag_part], axis=2) * factor
    return stacked.reshape(stacked.shape[0], stacked.shape[1], -1).astype(jnp.bfloat16)


def apply_block(kernel_rows, maps_rows, cos_table, sin_table):

    def product(left_op, right_op):
        return jnp.einsum(
            "sycdp,ysdx->yscpx", left_op, right_op, preferred_element_type=jnp.float32
        )

    mixed_real = product(kernel_rows[:, :, 0], maps_rows[:, :, 0]) - product(
        kernel_rows[:, :, 1], maps_rows[:, :, 1]
    )
    mixed_imag = product(kernel_rows[:, :, 0], maps_rows[:, :, 1]) + product(
        kernel_rows[:, :, 1], maps_rows[:, :, 0]
    )

    def apply_table(values_in, table):
        return jnp.einsum("yscpx,px->yscx", values_in, table, precision=lax.Precision.HIGHEST)

    out_real = apply_table(mixed_real, cos_table) - apply_table(mixed_imag, sin_table)
    out_imag = apply_table(mixed_real, sin_table) + apply_table(mixed_imag, cos_table)
    return jnp.stack([out_real, out_imag], axis=2).astype(jnp.bfloat16)


def shards(basis, picks, coil_maps):
    coil_share = COILS // lax.axis_size("col")
    own_rows = coil_share * KSIZE * KSIZE
    col_index = lax.axis_index("col")
    chosen = jax.vmap(lambda values_in, columns: jnp.take(values_in, columns, axis=2))(basis, picks)
    shard_part = lax.all_gather(chosen, "col", axis=3, tiled=True)
    left_rows = lax.dynamic_slice_in_dim(shard_part, col_index * own_rows, own_rows, 2)
    gram = outer_gram(left_rows, shard_part)
    kernels = kernel_sums(gram)
    span = 2 * KSIZE - 1
    cos_table, sin_table = phase_tables(span, IMG)
    factor = 1.0 / (2.0 * RANK * KSIZE * KSIZE)
    width_y = IMG // lax.axis_size("slc")
    local_rows = column_transform(kernels, cos_table, sin_table, factor)
    columns_all = lax.all_to_all(local_rows, "slc", split_axis=1, concat_axis=0, tiled=True)
    total_slices = columns_all.shape[0]
    kernels_y = columns_all.reshape(total_slices, width_y, 2, coil_share, COILS, span)
    per_block = 8
    result = jnp.zeros((width_y, total_slices, 2, coil_share, IMG), jnp.bfloat16)

    def one_block(block_index, result_now):
        first_row = block_index * per_block
        kernel_rows = lax.dynamic_slice_in_dim(kernels_y, first_row, per_block, 0)
        maps_rows = lax.dynamic_slice_in_dim(coil_maps, first_row, per_block, 1)
        block_out = apply_block(kernel_rows, maps_rows, cos_table, sin_table)
        return lax.dynamic_update_slice_in_dim(result_now, block_out, first_row, 1)

    return lax.fori_loop(0, total_slices // per_block, one_block, result)


def solution(mesh):
    placed = (P("slc", None, None, "col"), P("slc", "col"), P("slc", None, None, None, None))
    return jax.shard_map(
        shards,
        mesh=mesh,
        in_specs=placed,
        out_specs=P("slc", None, None, "col", None),
        check_vma=False,
    )
```

profile of v0, /device:TPU:13, one launch (start us, length us, event | category | flops | bytes accessed | tf_op | source)
XLA Modules:
  0.0 597.0 jit_solution(11189892527130384715)
XLA Ops:
  6.5 0.7 fusion.83
  7.2 0.7 and_reduce_fusion
  8.0 16.7 %gather_fusion = bf16[304,2,1152]{2,0,1:T(8,128)(2,1)S(1)} fusion(bf16[1,2,1152,1728]{2,3,1,0:T(8,128)(2,1)} %param.5, s32[304]{0:T(512)S(1)} %fusion.61), kind=kCustom, calls=%fused_computation | custom fusion | bytes 2804096 | tf_op jit(solution)/shard_map/vmap(jit(_take))/gather | solution.py:90
  24.7 1.3 bitcast_select_fusion
  26.0 42.1 %all-gather.2.cloned.1.call-done = bf16[1,2,1152,608]{2,3,1,0:T(8,128)(2,1)} async-done(((bf16[1,2,1152,304]{2,3,1,0:T(8,128)(2,1)}), bf16[1,2,1152,608]{2,3,1,0:T(8,128)(2,1)}) %all-gather.2.cloned.1.call-update) | async-done | bytes 2801680 | tf_op jit(solution)/shard_map/all_gather | solution.py:91
  68.1 3.2 fusion.35
  71.4 1.5 convolution_add_fusion.1
  72.9 40.0 %stack.42 = f32[1,1,16,6,6,32,6,6]{7,6,5,4,3,2,1,0:T(8,128)} reshape(f32[576,1152]{1,0:T(8,128)S(1)} %convolution_add_fusion.1) | data formatting | bytes 5308416 | tf_op jit(solution)/shard_map/stack | solution.py:41
  112.9 49.5 %copy.29 = f32[1,1,16,6,6,32,6,6]{5,6,3,7,4,2,1,0:T(8,128)} copy(f32[1,1,16,6,6,32,6,6]{7,6,5,4,3,2,1,0:T(8,128)} %stack.42) | data formatting | bytes 5308416 | tf_op jit(solution)/shard_map/stack | solution.py:41
  162.4 1.4 fusion.34
  163.8 0.3 copy-done.3
  164.1 1.5 convolution_subtract_fusion.1
  165.6 40.3 %stack.43 = f32[1,1,16,6,6,32,6,6]{7,6,5,4,3,2,1,0:T(8,128)} reshape(f32[576,1152]{1,0:T(8,128)S(1)} %convolution_subtract_fusion.1) | data formatting | bytes 5308416 | tf_op jit(solution)/shard_map/stack | solution.py:41
  206.0 49.3 %copy.30 = f32[1,1,16,6,6,32,6,6]{5,6,3,7,4,2,1,0:T(8,128)} copy(f32[1,1,16,6,6,32,6,6]{7,6,5,4,3,2,1,0:T(8,128)} %stack.43) | data formatting | bytes 5308416 | tf_op jit(solution)/shard_map/stack | solution.py:41
  255.3 23.2 %fusion.24 = f32[11,2,16,6,32,6]{4,0,5,3,2,1:T(8,128)S(1)} fusion(f32[1,1,16,6,6,32,6,6]{5,6,3,7,4,2,1,0:T(8,128)} %copy.30, f32[1,1,16,6,6,32,6,6]{5,6,3,7,4,2,1,0:T(8,128)} %copy.29, s32[6,6]{1,0:T(8,128)S(1)} %subtract_add_fusion), kind=kOutput, calls=%fused_computation.45 | convolution fusion | flops 176505232 | bytes 6930576 | tf_op jit(solution)/shard_map/srcaxdby,abp,xyq->srcdpq/dot_general | solution.py:48
  278.5 6.9 %fusion.25 = f32[1,2,16,32,11,11]{3,5,2,1,4,0:T(8,128)S(1)} fusion(f32[11,2,16,6,32,6]{4,0,5,3,2,1:T(8,128)S(1)} %fusion.24, s32[6,6]{1,0:T(8,128)S(1)} %subtract_add_fusion), kind=kOutput, calls=%fused_computation.48 | convolution fusion | flops 53526924 | bytes 2117776 | tf_op jit(solution)/shard_map/srcaxdby,abp,xyq->srcdpq/dot_general | solution.py:48
  285.4 0.2 slice_bitcast_fusion
  285.6 4.7 fusion.32
  290.3 5.0 fusion.30
  295.3 4.7 subtract_bitcast_fusion
  300.0 5.0 add_bitcast_fusion
  304.9 0.7 fusion.23
  305.7 3.4 copy.36
  309.1 5.0 convert_element_type.39
  314.1 10.1 %copy.37 = bf16[1,128,11264]{2,0,1:T(2,128)(2,1)} copy(bf16[1,128,11264]{1,2,0:T(8,128)(2,1)S(1)} %convert_element_type.39) | data formatting | bytes 5767168 | tf_op jit(solution)/shard_map/convert_element_type | solution.py:61
  324.2 0.5 broadcast.125
  324.7 17.7 %reduce.14 = bf16[128,11264]{1,0:T(8,128)(2,1)S(1)} reduce(bf16[128,1,11264]{2,1,0:T(2,128)(2,1)} %bitcast.151, bf16[]{:T(256)} %broadcast.125), dimensions={1}, to_apply=%bitcast.120.reduce_sub_computation | reduce | bytes 5767170
  342.4 4.1 reshape.178
  346.5 6.8 %all-to-all-start = ((bf16[16,2,45056]{2,1,0:T(2,128)(2,1)}), bf16[16,2,45056]{2,1,0:T(2,128)(2,1)S(1)}, u32[]{:S(2)}, u32[]{:S(2)}) async-start(bf16[16,2,45056]{2,1,0:T(2,128)(2,1)} %reshape.178), calls=%async_computation | async-start | bytes 5767168 | tf_op jit(solution)/shard_map/all_to_all | solution.py:100
  353.4 64.2 %all-to-all-done = bf16[16,2,45056]{2,1,0:T(2,128)(2,1)S(1)} async-done(((bf16[16,2,45056]{2,1,0:T(2,128)(2,1)}), bf16[16,2,45056]{2,1,0:T(2,128)(2,1)S(1)}, u32[]{:S(2)}, u32[]{:S(2)}) %all-to-all-start) | async-done | bytes 2883616 | tf_op jit(solution)/shard_map/all_to_all | solution.py:100
  417.6 7.4 %reshape.179 = bf16[128,1,11264]{2,1,0:T(2,128)(2,1)} reshape(bf16[16,2,45056]{2,1,0:T(2,128)(2,1)S(1)} %all-to-all-done) | data formatting | bytes 5767168
  425.0 17.3 %bitcast_reduce_fusion = bf16[128,11264]{1,0:T(8,128)(2,1)S(1)} fusion(bf16[128,1,11264]{2,1,0:T(2,128)(2,1)} %reshape.179), kind=kLoop, calls=%fused_computation.117 | loop fusion | bytes 5767168 | tf_op jit(solution)/shard_map/all_to_all | solution.py:100
  442.3 76.7 %reshape.150 = bf16[16,8,2,16,32,11]{5,4,3,2,1,0:T(8,128)(2,1)} reshape(bf16[128,11264]{1,0:T(8,128)(2,1)S(1)} %bitcast_reduce_fusion) | data formatting | bytes 5767168 | tf_op jit(solution)/shard_map/reshape | solution.py:102
  519.0 38.7 %copy.38 = bf16[16,8,2,16,32,11]{4,3,5,0,1,2:T(8,128)(2,1)} copy(bf16[16,8,2,16,32,11]{5,4,3,2,1,0:T(8,128)(2,1)} %reshape.150) | data formatting | bytes 5767168
  557.7 1.1 broadcast_in_dim.20
  558.9 30.7 %while.16 = (s32[]{:T(128)}, bf16[8,16,2,16,128]{4,3,2,1,0:T(8,128)(2,1)}, bf16[16,8,2,16,32,11]{4,3,5,0,1,2:T(8,128)(2,1)}, bf16[8,16,2,32,128]{4,3,2,1,0:T(8,1...) while((s32[]{:T(128)}, ...), condition=%wide.region_1.2_spmd.clone.clone.clone, body=%wide.region_0.1_spmd.clone.clone.clone.sunk | while | flops 384584960 | bytes 88638744 | solution.py:113
  559.2 3.6 fusion.87
  562.8 3.7 convolution_add_fusion.3
  566.6 1.6 fusion.88
  568.4 3.7 multiply_reduce_fusion.5
  572.0 1.5 fusion.89
  573.5 0.9 maximum_dynamic-update-slice_fusion.2
  574.4 3.6 fusion.87
  578.0 3.7 convolution_add_fusion.3
  581.8 1.6 fusion.88
  583.6 3.7 multiply_reduce_fusion.5
  587.2 1.5 fusion.89
  588.7 0.9 maximum_dynamic-update-slice_fusion.2
  (29 shorter events, 0.4 us)
Async XLA Ops:
  6.5 61.6 %all-gather.2.cloned.1.call-start = ((), (), s32[]{:S(2)}) async-start(), calls=%async_computation.1 | async-start | bytes 4202496 | tf_op jit(solution)/shard_map/all_gather | solution.py:91
  68.1 3.2 copy-start.1
  112.9 49.5 %copy-start.2 = (bf16[1,2,1152,608]{2,3,1,0:T(8,128)(2,1)S(1)}, bf16[1,2,1152,608]{2,3,1,0:T(8,128)(2,1)}, u32[]{:S(2)}) copy-start(bf16[1,2,1152,608]{2,3,1,0:T(8,128)(2,1)} %all-gather.2.cloned.1.call-done) | copy-start | bytes 8404996
  162.4 1.8 copy-start.3
  346.5 71.0 %all-to-all-start = ((bf16[16,2,45056]{2,1,0:T(2,128)(2,1)}), bf16[16,2,45056]{2,1,0:T(2,128)(2,1)S(1)}, u32[]{:S(2)}, u32[]{:S(2)}) async-start(bf16[16,2,45056]{2,1,0:T(2,128)(2,1)} %reshape.178), calls=%async_computation | async-start | bytes 5767168 | tf_op jit(solution)/shard_map/all_to_all | solution.py:100
  519.0 39.9 %copy-start = (bf16[8,16,2,32,128]{4,3,2,1,0:T(8,128)(2,1)S(1)}, bf16[8,16,2,32,128]{4,3,2,1,0:T(8,128)(2,1)}, u32[]{:S(2)}) copy-start(bf16[8,16,2,32,128]{4,3,2,1,0:T(8,128)(2,1)} %param.7) | copy-start | bytes 6291460
  559.2 7.4 %slice-start = ((s8[11534336]{0:T(1024)(128)(4,1)}), s8[4194304]{0:T(1024)(128)(4,1)S(1)}, s32[]{:S(2)}) async-start(s8[11534336]{0:T(1024)(128)(4,1)} %bitcast.149), calls=%async_computation.2 | async-start | bytes 8388608 | tf_op jit(solution)/shard_map/while
  559.2 7.4 %slice-start.1 = ((s8[11534336]{0:T(1024)(128)(4,1)}), s8[4194304]{0:T(1024)(128)(4,1)S(1)}, s32[]{:S(2)}) async-start(s8[11534336]{0:T(1024)(128)(4,1)} %bitcast.149), calls=%async_computation.3 | async-start | bytes 8388608 | tf_op jit(solution)/shard_map/while
  562.8 3.8 slice-start.2
  574.4 7.3 %slice-start = ((s8[11534336]{0:T(1024)(128)(4,1)}), s8[4194304]{0:T(1024)(128)(4,1)S(1)}, s32[]{:S(2)}) async-start(s8[11534336]{0:T(1024)(128)(4,1)} %bitcast.149), calls=%async_computation.2 | async-start | bytes 8388608 | tf_op jit(solution)/shard_map/while
  574.4 7.3 %slice-start.1 = ((s8[11534336]{0:T(1024)(128)(4,1)}), s8[4194304]{0:T(1024)(128)(4,1)S(1)}, s32[]{:S(2)}) async-start(s8[11534336]{0:T(1024)(128)(4,1)} %bitcast.149), calls=%async_computation.3 | async-start | bytes 8388608 | tf_op jit(solution)/shard_map/while
  578.0 3.8 slice-start.2
Sparse Core Ops, SparseCore 0:
  26.1 41.9 all-gather.1
where the time goes:
time: 609 us; the launch traced here: 597 us
  local copies, waits for them, and re-layouts  361 us (59%)
  waiting for transfers between devices  106 us (17%)
  matrix products  82.3 us (14%)
  other arithmetic  26.2 us (4%)
  between operations  14.1 us (2%)
  starting transfers between devices  6.85 us (1%)
    another operation x4, local copies, waits for them, and re-layouts, outer_gram(): return jnp.stack([real_part, imag_part], axis=1)  179 us
    reshape x1, local copies, waits for them, and re-layouts, shards(): columns_all.reshape(total_slices, width_y, 2, coil_share, COILS, span)  76.7 us
    all_to_all x1, waiting for transfers between devices, shards(): lax.all_to_all(local_rows, 'slc', split_axis=1, concat_axis=0, tiled=True)  64.2 us
    unnamed x12, local copies, waits for them, and re-layouts  51.1 us
    all_gather x1, waiting for transfers between devices, shards(): shard_part = lax.all_gather(chosen, 'col', axis=3, tiled=True)  42.1 us
    dot_general x2, matrix products, kernel_sums(): jnp.einsum('srcaxdby,abp,xyq->srcdpq', blocks, shifts, shifts, precision=...  30.1 us
    dot_general x8, matrix products, product(): jnp.einsum('sycdp,ysdx->yscpx', left_op, right_op, preferred_element_type...  25.3 us
    dot_general x4, matrix products, apply_table(): jnp.einsum('scdpq,qy->sycdp', values_in, table, precision=lax.Precision.H...  19.3 us
  transfers between devices with their start and end apart: 2, of which 2 were waited for; matrix products, arithmetic and copies ran while one was open for 0% of the time, Pallas kernels for 0%

commit v1 on v0

v1 whole, which is shorter than its diff:
```python
import functools
import math

import jax
import jax.numpy as jnp
from jax import lax
from jax.experimental import pallas as pl
from jax.experimental.pallas import tpu as pltpu
from jax.sharding import PartitionSpec as P

COILS = 32
KSIZE = 6
SPAN = 2 * KSIZE - 1
SLOTS = SPAN + 1
CENTRE = KSIZE - 1
PAIR = 2 * COILS


def dot_nn(left, right):
    return jnp.dot(left, right, preferred_element_type=jnp.float32)


def dot_nt(left, right):
    return lax.dot_general(
        left, right, (((1,), (1,)), ((), ())), preferred_element_type=jnp.float32
    )


def gram_kernel(
    factor, share, col_ref, basis_ref, picks_ref, own_ref, other_ref, hot, order, x, xa, xb, yr, yi, tacc
):
    keep, block = hot.shape
    rows = order.shape[0]
    side = KSIZE * share
    parts = COILS // share
    lanes = lax.broadcasted_iota(jnp.int32, (keep, block), 1)
    hot[...] = (lanes == picks_ref[...]).astype(jnp.float32).astype(jnp.bfloat16)
    source = lax.broadcasted_iota(jnp.int32, (COILS, rows), 1)
    coil = lax.broadcasted_iota(jnp.int32, (COILS, rows), 0)
    gap = source - coil * (KSIZE * KSIZE)

    def fill(spot, carry):
        at = pl.multiple_of(spot * COILS, COILS)
        order[pl.ds(at, COILS), :] = (gap == spot).astype(jnp.float32).astype(jnp.bfloat16)
        return carry

    lax.fori_loop(0, KSIZE * KSIZE, fill, 0)
    chunk = KSIZE * COILS

    def choose(ri, carry):
        windows = dot_nn(hot[...], basis_ref[ri]).astype(jnp.bfloat16)

        def permute(step, inner):
            at = pl.multiple_of(step * chunk, chunk)
            x[ri, pl.ds(at, chunk), :] = dot_nt(order[pl.ds(at, chunk), :], windows).astype(
                jnp.bfloat16
            )
            return inner

        return lax.fori_loop(0, rows // chunk, permute, carry)

    lax.fori_loop(0, 2, choose, 0)

    zeros = jnp.zeros((PAIR, keep), jnp.bfloat16)
    for a in range(KSIZE):
        for ref in (xa, xb):
            ref[a, :PAIR, :] = zeros
            ref[a, (KSIZE + 1) * PAIR :, :] = zeros
        for b in range(KSIZE):
            at = (a * KSIZE + b) * COILS
            to = (b + 1) * PAIR
            real = x[0, at : at + COILS, :]
            imag = x[1, at : at + COILS, :]
            xa[a, to : to + COILS, :] = real
            xa[a, to + COILS : to + PAIR, :] = -imag
            xb[a, to : to + COILS, :] = imag
            xb[a, to + COILS : to + PAIR, :] = real
            for h in range(parts):
                row = h * side + a * share
                yr[b, row : row + share, :] = x[0, at + h * share : at + (h + 1) * share, :]
                yi[b, row : row + share, :] = x[1, at + h * share : at + (h + 1) * share, :]

    def blocks(a2, carry):
        tacc[a2] = jnp.zeros(tacc.shape[1:], jnp.float32)
        for b in range(KSIZE):
            if (CENTRE - b) % 2 == 0:
                low, high, off = PAIR, (KSIZE + 1) * PAIR, (CENTRE - b) * PAIR
            else:
                low, high, off = 0, (KSIZE + 2) * PAIR, (CENTRE - 1 - b) * PAIR
            tacc[a2, :, off : off + high - low] += dot_nt(yr[b], xa[a2, low:high, :]) + dot_nt(
                yi[b], xb[a2, low:high, :]
            )
        return carry

    lax.fori_loop(0, KSIZE, blocks, 0)

    own = col_ref[0]
    for ref, part in ((own_ref, own), (other_ref, parts - 1 - own)):
        for p in range(SPAN):
            total = None
            for a in range(max(0, CENTRE - p), min(KSIZE, KSIZE + CENTRE - p)):
                at = pl.multiple_of(part * side + a * share, share)
                term = tacc[a + p - CENTRE, pl.ds(at, share), :]
                total = term if total is None else total + term
            ref[p * share : (p + 1) * share, :] = total * factor


def join_kernel(own_ref, got_ref, out_ref):
    total = own_ref[...] + got_ref[...]
    high = total.astype(jnp.bfloat16)
    left = total - high.astype(jnp.float32)
    last = SPAN * PAIR
    out_ref[...] = high
    mid = CENTRE * PAIR
    out_ref[:, last:] = left[:, mid : mid + PAIR].astype(jnp.bfloat16)


def apply_kernel(
    width, share, kernels_ref, phase_ref, cos_ref, sin_ref, maps_ref, out_ref, high, low
):
    @pl.when(pl.program_id(0) == 0)
    def _():
        phase = phase_ref[...]
        phase_high = phase.astype(jnp.bfloat16)
        phase_low = (phase - phase_high.astype(jnp.float32)).astype(jnp.bfloat16)
        from_lane = lax.broadcasted_iota(jnp.int32, (phase.shape[1], width * PAIR), 0)
        to_lane = lax.broadcasted_iota(jnp.int32, (phase.shape[1], width * PAIR), 1)
        spread = (from_lane == to_lane // COILS).astype(jnp.float32).astype(jnp.bfloat16)
        row = lax.broadcasted_iota(jnp.int32, high.shape, 0)
        lane = lax.broadcasted_iota(jnp.int32, high.shape, 1)
        same = row % COILS == lane % COILS
        high[...] = jnp.where(same, dot_nn(phase_high, spread), 0.0).astype(jnp.bfloat16)
        low[...] = jnp.where(same, dot_nn(phase_low, spread), 0.0).astype(jnp.bfloat16)

    kernels = kernels_ref[0]
    image = (dot_nn(kernels, high[...]) + dot_nn(kernels, low[...])).astype(jnp.bfloat16)
    cos_x = cos_ref[...]
    sin_x = sin_ref[...]
    length = cos_x.shape[1]
    for y in range(width):
        real = maps_ref[y, 0, 0]
        imag = maps_ref[y, 0, 1]
        both = jnp.concatenate(
            [jnp.concatenate([real, imag], axis=1), jnp.concatenate([-imag, real], axis=1)], axis=0
        )
        mixed = dot_nn(image[:, y * PAIR : (y + 1) * PAIR], both)
        mixed_real = mixed[:, :length]
        mixed_imag = mixed[:, length:]
        out_real = mixed_real * cos_x - mixed_imag * sin_x
        out_imag = mixed_real * sin_x + mixed_imag * cos_x
        for ri, value in ((0, out_real), (1, out_imag)):
            total = value[:share]
            for p in range(1, SPAN):
                total = total + value[p * share : (p + 1) * share]
            out_ref[y, 0, ri] = total.astype(jnp.bfloat16)


def shards(basis, picks, coil_maps):
    n_col = lax.axis_size("col")
    share = COILS // n_col
    length = coil_maps.shape[-1]
    width = coil_maps.shape[0]
    slices = coil_maps.shape[1]
    rows, block = basis.shape[2:]
    keep = picks.shape[1]
    factor = 1.0 / (2.0 * keep * n_col * KSIZE * KSIZE)
    high_rows = SPAN * share
    lanes = SLOTS * PAIR
    vmem = pl.BlockSpec(memory_space=pltpu.VMEM)
    bf16 = jnp.bfloat16

    windows = jnp.transpose(basis[0], (0, 2, 1))
    col = lax.axis_index("col").astype(jnp.int32).reshape(1)
    part = jax.ShapeDtypeStruct((high_rows, lanes), jnp.float32)
    own, other = pl.pallas_call(
        functools.partial(gram_kernel, factor, share),
        out_shape=(part, part),
        in_specs=[pl.BlockSpec(memory_space=pltpu.SMEM), vmem, vmem],
        out_specs=(vmem, vmem),
        scratch_shapes=[
            pltpu.VMEM((keep, block), bf16),
            pltpu.VMEM((rows, rows), bf16),
            pltpu.VMEM((2, rows, keep), bf16),
            pltpu.VMEM((KSIZE, (KSIZE + 2) * PAIR, keep), bf16),
            pltpu.VMEM((KSIZE, (KSIZE + 2) * PAIR, keep), bf16),
            pltpu.VMEM((KSIZE, KSIZE * COILS, keep), bf16),
            pltpu.VMEM((KSIZE, KSIZE * COILS, keep), bf16),
            pltpu.VMEM((KSIZE, KSIZE * COILS, lanes), jnp.float32),
        ],
        compiler_params=pltpu.CompilerParams(vmem_limit_bytes=60 * 2**20),
        name="gram",
    )(col, windows, picks.reshape(keep, 1))

    got = lax.ppermute(other, "col", [(i, n_col - 1 - i) for i in range(n_col)])
    kernels = pl.pallas_call(
        join_kernel,
        out_shape=jax.ShapeDtypeStruct((high_rows, lanes), bf16),
        in_specs=[vmem, vmem],
        out_specs=vmem,
        name="join",
    )(own, got)
    gathered = lax.all_gather(kernels, "slc", axis=0)

    row = lax.broadcasted_iota(jnp.int32, (lanes, 128), 0)
    lane = lax.broadcasted_iota(jnp.int32, (lanes, 128), 1)
    slot = row // PAIR
    offset = jnp.where(slot == SPAN, 0, slot - CENTRE)
    column = lax.axis_index("slc") * width + lane // 2
    angle = (offset * column % length).astype(jnp.float32) * (2.0 * math.pi / length)
    from_imag = row // COILS % 2
    to_imag = lane % 2
    phase = jnp.where(from_imag == to_imag, jnp.cos(angle), jnp.sin(angle))
    phase = jnp.where((from_imag == 1) & (to_imag == 0), -phase, phase)

    spot = lax.broadcasted_iota(jnp.int32, (high_rows, length), 0) // share - CENTRE
    place = lax.broadcasted_iota(jnp.int32, (high_rows, length), 1)
    turn = (spot * place % length).astype(jnp.float32) * (2.0 * math.pi / length)

    whole = lambda shape: pl.BlockSpec(shape, lambda s: (0,) * len(shape))
    return pl.pallas_call(
        functools.partial(apply_kernel, width, share),
        grid=(slices,),
        out_shape=jax.ShapeDtypeStruct((width, slices, 2, share, length), bf16),
        in_specs=[
            pl.BlockSpec((1, high_rows, lanes), lambda s: (s, 0, 0)),
            whole((lanes, 128)),
            whole((high_rows, length)),
            whole((high_rows, length)),
            pl.BlockSpec((width, 1, 2, COILS, length), lambda s: (0, s, 0, 0, 0)),
        ],
        out_specs=pl.BlockSpec((width, 1, 2, share, length), lambda s: (0, s, 0, 0, 0)),
        scratch_shapes=[
            pltpu.VMEM((lanes, width * PAIR), bf16),
            pltpu.VMEM((lanes, width * PAIR), bf16),
        ],
        name="apply",
    )(gathered, phase, jnp.cos(turn), jnp.sin(turn), coil_maps)


def solution(mesh):
    placed = (P("slc", None, None, "col"), P("slc", "col"), P("slc", None, None, None, None))
    return jax.shard_map(
        shards,
        mesh=mesh,
        in_specs=placed,
        out_specs=P("slc", None, None, "col", None),
        check_vma=False,
    )
```

time: 609 us -> 127 us (0.21)
  the two profiles are of different devices: /device:TPU:13 before, /device:TPU:0 now
where the time goes in v1:
time: 127 us
  waiting for transfers between devices  60.3 us (47%)
  Pallas kernels  43 us (34%)
  between operations  13.4 us (11%)
  other arithmetic  4.99 us (4%)
  starting transfers between devices  2.89 us (2%)
  local copies, waits for them, and re-layouts  2.28 us (2%)
    all_gather x1, waiting for transfers between devices, shards(): gathered = lax.all_gather(kernels, 'slc', axis=0)  47.7 us
    pallas_call x1, Pallas kernels, shards(): pl.pallas_call(functools.partial(gram_kernel, factor, share), out_shape=(...  24.1 us
    pallas_call x1, Pallas kernels, shards(): pl.pallas_call(functools.partial(apply_kernel, width, share), grid=(slice...  16.9 us
    ppermute x1, waiting for transfers between devices, shards(): got = lax.ppermute(other, 'col', [(i, n_col - 1 - i) for i in range(n_col)])  12.5 us
    select_n x1, other arithmetic, shards(): phase = jnp.where((from_imag == 1) & (to_imag == 0), -phase, phase)  3.78 us
    ppermute x1, starting transfers between devices, shards(): got = lax.ppermute(other, 'col', [(i, n_col - 1 - i) for i in range(n_col)])  2.89 us
  transfers between devices with their start and end apart: 2, of which 2 were waited for; matrix products, arithmetic and copies ran while one was open for 4% of the time, Pallas kernels for 0%

profile of v1, /device:TPU:0, one launch (start us, length us, event | category | flops | bytes accessed | tf_op | source)
XLA Modules:
  0.0 126.9 jit_solution(7136202463287652002)
XLA Ops:
  6.5 0.0 all-gather.3.cloned.1.call-start
  6.5 1.5 %copy.4.picks_ref = s32[304,1]{1,0:T(8,128)} copy(s32[304,1]{0,1:T(1,128)} %bitcast.8) | data formatting | bytes 2432 | tf_op jit(solution)/shard_map/reshape | solution.py:192
  8.0 24.1 %gram.1 = (f32[176,768]{1,0:T(8,128)}, f32[176,768]{1,0:T(8,128)}) custom-call(s32[1]{0:T(128)} %bitcast.col_ref, bf16[2,1728,1152]{2,1,0:T(8,128)(2,1)} %bitcast.6, s32[304,1]{1,0:T(8,128)} %copy.4.picks_ref), custom_call_target="tpu_custom_call" | custom-call | tf_op jit(solution)/shard_map/gram/pallas_call | solution.py:175
  32.1 2.9 %collective-permute-start = (f32[176,768]{1,0:T(8,128)}, f32[176,768]{1,0:T(8,128)S(1)}, u32[]{:S(2)}, u32[]{:S(2)}) collective-permute-start(f32[176,768]{1,0:T(8,128)} %get-tuple-element.8), channel_id=1, source_target_pairs={{0,1},{1,0},{2,3},{3,2},{4,5},{5,4},{6,7},{7,6},{8,9},{9,8},{10,11... | collective-permute-start | bytes 1622024 | tf_op jit(solution)/shard_map/ppermute | solution.py:194
  35.0 12.5 %collective-permute-done.got_ref = f32[176,768]{1,0:T(8,128)S(1)} collective-permute-done((f32[176,768]{1,0:T(8,128)}, f32[176,768]{1,0:T(8,128)S(1)}, u32[]{:S(2)}, u32[]{:S(2)}) %collective-permute-start) | collective-permute-done | bytes 540704 | tf_op jit(solution)/shard_map/ppermute | solution.py:194
  47.5 0.0 copy-start
  47.5 0.8 copy-done
  48.3 2.0 %join.1 = bf16[176,768]{1,0:T(8,128)(2,1)} custom-call(f32[176,768]{1,0:T(8,128)} %get-tuple-element.7.own_ref, f32[176,768]{1,0:T(8,128)} %copy-done), custom_call_target="tpu_custom_call" | custom-call | tf_op jit(solution)/shard_map/join/pallas_call | solution.py:195
  50.3 0.0 all-gather.3.cloned.1.call-update
  50.4 1.2 fusion.10
  51.6 3.8 %negate_select_fusion.phase_ref = f32[768,128]{1,0:T(8,128)} fusion(s32[128]{0:T(128)S(1)} %get-tuple-element.19, s32[128]{0:T(128)S(1)} %get-tuple-element.21, s32[]{:T(128)S(6)} %mul.25, s32[768]{0:T(1024)S(1)} %get-tuple-element.12, s32[768]{0:T(1024)S(1)} %get-tuple-element.15, s32[128]{0:T(128)S(1)} %get-tuple-element.20, s32[128]{0:T(128)S(1)} %get-tuple-element.22, ...), kind=kLoop, calls=%fused_computation.3 | loop fusion | flops 3932160 | bytes 409348 | tf_op jit(solution)/shard_map/jit(_where)/select_n | solution.py:213
  55.4 47.7 %all-gather.3.cloned.1.call-done = bf16[2816,768]{1,0:T(8,128)(2,1)} async-done(((bf16[176,768]{1,0:T(8,128)(2,1)}), bf16[2816,768]{1,0:T(8,128)(2,1)}) %all-gather.3.cloned.1.call-update) | async-done | bytes 4325392 | tf_op jit(solution)/shard_map/all_gather | solution.py:202
  103.1 16.9 %apply.1 = bf16[8,16,2,16,128]{4,3,2,1,0:T(8,128)(2,1)} custom-call(bf16[16,176,768]{2,1,0:T(8,128)(2,1)} %bitcast.7, f32[768,128]{1,0:T(8,128)} %negate_select_fusion.phase_ref, f32[176,128]{1,0:T(8,128)} %get-tuple-element.10.cos_ref, f32[176,128]{1,0:T(8,128)} %get-tuple-element.9.sin_ref, bf16[8,16,2,32,128]{4,3,2,1,0:T(8,128)(2,1)} %maps_ref.1), custom_call_target="tpu_custom_call" | custom-call | tf_op jit(solution)/shard_map/apply/pallas_call | solution.py:220
  (8 shorter events, 0.0 us)
Async XLA Ops:
  6.5 96.6 %all-gather.3.cloned.1.call-start = ((), (), s32[]{:S(2)}) async-start(), calls=%async_computation | async-start | bytes 4595712 | tf_op jit(solution)/shard_map/all_gather | solution.py:202
  32.1 15.4 %collective-permute-start = (f32[176,768]{1,0:T(8,128)}, f32[176,768]{1,0:T(8,128)S(1)}, u32[]{:S(2)}, u32[]{:S(2)}) collective-permute-start(f32[176,768]{1,0:T(8,128)} %get-tuple-element.8), channel_id=1, source_target_pairs={{0,1},{1,0},{2,3},{3,2},{4,5},{5,4},{6,7},{7,6},{8,9},{9,8},{10,11... | collective-permute-start | bytes 1622024 | tf_op jit(solution)/shard_map/ppermute | solution.py:194
  47.5 0.8 copy-start
Sparse Core Ops, SparseCore 0:
  50.5 52.5 all-gather.2

commit v2 on v1

--- a/solution.py
+++ b/solution.py
@@ -113,6 +113,89 @@
     out_ref[...] = high
     mid = CENTRE * PAIR
     out_ref[:, last:] = left[:, mid : mid + PAIR].astype(jnp.bfloat16)
+
+
+def spread_kernel(in_ref, out_ref, local_sem, send, got):
+    chips = lax.axis_size("slc") // 2
+    me = lax.axis_index("slc")
+    core = me % 2
+    column = me // 2 // 2
+    side = me // 2 % 2
+    spot = column + side * (chips - 1 - 2 * column)
+
+    def at(position):
+        position = (position + 2 * chips) % chips
+        far = position // (chips // 2)
+        near = position + far * (chips - 1 - 2 * position)
+        return (2 * near + far) * 2 + core
+
+    ahead, behind, twin = at(spot + 1), at(spot - 1), me + 1 - 2 * core
+    barrier = pltpu.get_barrier_semaphore()
+    for peer in (ahead, behind, twin):
+        pl.semaphore_signal(
+            barrier, inc=1, device_id={"slc": peer}, device_id_type=pl.DeviceIdType.MESH
+        )
+    pl.semaphore_wait(barrier, 3)
+
+    forward = chips // 2
+    backward = chips - 1 - forward
+    rows = in_ref.shape[0]
+    cut = (rows // 2 + 15) // 16 * 16
+    pieces = ((0, cut), (cut, rows - cut))
+    ring_ahead, ring_behind, across = 0, forward, forward + backward
+
+    def copy(source, slot, piece, index, peer):
+        start, size = pieces[piece]
+        target = out_ref.at[slot, pl.ds(start, size), :]
+        taken = target if source is None else source.at[pl.ds(start, size), :]
+        return pltpu.make_async_remote_copy(
+            src_ref=taken,
+            dst_ref=target,
+            send_sem=send.at[index, piece],
+            recv_sem=got.at[index, piece],
+            device_id={"slc": peer},
+            device_id_type=pl.DeviceIdType.MESH,
+        )
+
+    local = pltpu.make_async_copy(in_ref, out_ref.at[me], local_sem)
+    sent = []
+
+    def launch(*what):
+        one = copy(*what)
+        one.start()
+        sent.append(one)
+
+    for piece in range(2):
+        launch(in_ref, me, piece, ring_ahead, ahead)
+        launch(in_ref, me, piece, ring_behind, behind)
+    for piece in range(2):
+        launch(in_ref, me, piece, across, twin)
+    local.start()
+    for step in range(forward):
+        for piece in range(2):
+            slot = at(spot - 1 - step)
+            copy(None, slot, piece, ring_ahead + step, behind).wait_recv()
+            if step + 1 < forward:
+                launch(None, slot, piece, ring_ahead + step + 1, ahead)
+            launch(None, slot, piece, across + 1 + step, twin)
+            if step < backward:
+                slot = at(spot + 1 + step)
+                copy(None, slot, piece, ring_behind + step, ahead).wait_recv()
+                if step + 1 < backward:
+                    launch(None, slot, piece, ring_behind + step + 1, behind)
+                launch(None, slot, piece, across + 1 + forward + step, twin)
+    for index in range(chips):
+        for piece in range(2):
+            if index == 0:
+                slot = twin
+            elif index <= forward:
+                slot = at(spot - index) + 1 - 2 * core
+            else:
+                slot = at(spot + index - forward) + 1 - 2 * core
+            copy(None, slot, piece, across + index, twin).wait_recv()
+    for one in sent:
+        one.wait_send()
+    local.wait()
 
 
 def apply_kernel(
@@ -199,7 +282,20 @@
         out_specs=vmem,
         name="join",
     )(own, got)
-    gathered = lax.all_gather(kernels, "slc", axis=0)
+    n_slc = lax.axis_size("slc")
+    gathered = pl.pallas_call(
+        spread_kernel,
+        out_shape=jax.ShapeDtypeStruct((n_slc, high_rows, lanes), bf16),
+        in_specs=[vmem],
+        out_specs=pl.BlockSpec(memory_space=pl.ANY),
+        scratch_shapes=[
+            pltpu.SemaphoreType.DMA,
+            pltpu.SemaphoreType.DMA((n_slc - 1, 2)),
+            pltpu.SemaphoreType.DMA((n_slc - 1, 2)),
+        ],
+        compiler_params=pltpu.CompilerParams(collective_id=0, has_side_effects=True),
+        name="spread",
+    )(kernels)
 
     row = lax.broadcasted_iota(jnp.int32, (lanes, 128), 0)
     lane = lax.broadcasted_iota(jnp.int32, (lanes, 128), 1)

time: 127 us -> 91.1 us (0.72)
  waiting for transfers between devices: 60.3 us -> 7.52 us
  Pallas kernels: 43 us -> 72.7 us
  between operations: 13.4 us -> 0.05 us
    all_gather x1 -> x0, waiting for transfers between devices: 47.7 us -> none  [shards(): gathered = lax.all_gather(kernels, 'slc', axis=0)]
    pallas_call x0 -> x1, Pallas kernels: none -> 29.8 us  [shards(): pl.pallas_call(spread_kernel, out_shape=jax.ShapeDtypeStruct((n_slc, high...]
    ppermute x1, waiting for transfers between devices: 12.5 us -> 7.52 us  [shards(): got = lax.ppermute(other, 'col', [(i, n_col - 1 - i) for i in range(n_col)])]
  transfers between devices with their start and end apart: 2 -> 1, of which waited for: 2 -> 1; matrix products, arithmetic and copies ran while one was open for 4% -> 6% of each run, Pallas kernels for 0% -> 0%
where the time goes in v2:
time: 91.1 us; the launch traced here: 90.5 us
  Pallas kernels  72.7 us (80%)
  waiting for transfers between devices  7.52 us (8%)
  other arithmetic  5 us (5%)
  starting transfers between devices  3 us (3%)
  local copies, waits for them, and re-layouts  2.27 us (2%)
    pallas_call x1, Pallas kernels, shards(): pl.pallas_call(spread_kernel, out_shape=jax.ShapeDtypeStruct((n_slc, high...  29.8 us
    pallas_call x1, Pallas kernels, shards(): pl.pallas_call(functools.partial(gram_kernel, factor, share), out_shape=(...  24 us
    pallas_call x1, Pallas kernels, shards(): pl.pallas_call(functools.partial(apply_kernel, width, share), grid=(slice...  17 us
    ppermute x1, waiting for transfers between devices, shards(): got = lax.ppermute(other, 'col', [(i, n_col - 1 - i) for i in range(n_col)])  7.52 us
    select_n x1, other arithmetic, shards(): phase = jnp.where((from_imag == 1) & (to_imag == 0), -phase, phase)  3.79 us
    ppermute x1, starting transfers between devices, shards(): got = lax.ppermute(other, 'col', [(i, n_col - 1 - i) for i in range(n_col)])  3 us
    pallas_call x1, Pallas kernels, shards(): pl.pallas_call(join_kernel, out_shape=jax.ShapeDtypeStruct((high_rows, la...  1.97 us
  transfers between devices with their start and end apart: 1, of which 1 were waited for; matrix products, arithmetic and copies ran while one was open for 6% of the time, Pallas kernels for 0%

profile of v2, /device:TPU:0, one launch (start us, length us, event | category | flops | bytes accessed | tf_op | source)
XLA Modules:
  0.0 90.5 jit_solution(13140298100876398201)
XLA Ops:
  0.0 1.5 %copy.4.picks_ref = s32[304,1]{1,0:T(8,128)} copy(s32[304,1]{0,1:T(1,128)} %bitcast.6) | data formatting | bytes 2432 | tf_op jit(solution)/shard_map/reshape | solution.py:275
  1.5 24.0 %gram.1 = (f32[176,768]{1,0:T(8,128)}, f32[176,768]{1,0:T(8,128)}) custom-call(s32[1]{0:T(128)} %bitcast.col_ref, bf16[2,1728,1152]{2,1,0:T(8,128)(2,1)} %bitcast.5, s32[304,1]{1,0:T(8,128)} %copy.4.picks_ref), custom_call_target="tpu_custom_call" | custom-call | tf_op jit(solution)/shard_map/gram/pallas_call | solution.py:258
  25.5 3.0 %collective-permute-start = (f32[176,768]{1,0:T(8,128)}, f32[176,768]{1,0:T(8,128)S(1)}, u32[]{:S(2)}, u32[]{:S(2)}) collective-permute-start(f32[176,768]{1,0:T(8,128)} %get-tuple-element.8), channel_id=1, source_target_pairs={{0,1},{1,0},{2,3},{3,2},{4,5},{5,4},{6,7},{7,6},{8,9},{9,8},{10,11... | collective-permute-start | bytes 1622024 | tf_op jit(solution)/shard_map/ppermute | solution.py:277
  28.5 1.2 %fusion.10 = (f32[176,128]{1,0:T(8,128)}, f32[176,128]{1,0:T(8,128)}) fusion(s32[176]{0:T(256)S(1)} %get-tuple-element.23, s32[176]{0:T(256)S(1)} %get-tuple-element.24, pred[176]{0:T(512)(128)(4,1)S(1)} %compare_and_fusion), kind=kLoop, calls=%fused_computation.26 | loop fusion | flops 360448 | bytes 181808 | tf_op jit(solution)/shard_map/sin | solution.py:333
  29.7 3.8 %negate_select_fusion.phase_ref = f32[768,128]{1,0:T(8,128)} fusion(s32[128]{0:T(128)S(1)} %get-tuple-element.19, s32[128]{0:T(128)S(1)} %get-tuple-element.21, s32[]{:T(128)S(6)} %mul.25, s32[768]{0:T(1024)S(1)} %get-tuple-element.12, s32[768]{0:T(1024)S(1)} %get-tuple-element.15, s32[128]{0:T(128)S(1)} %get-tuple-element.20, s32[128]{0:T(128)S(1)} %get-tuple-element.22, ...), kind=kLoop, calls=%fused_computation.3 | loop fusion | flops 3932160 | bytes 409348 | tf_op jit(solution)/shard_map/jit(_where)/select_n | solution.py:309
  33.5 7.5 %collective-permute-done.got_ref = f32[176,768]{1,0:T(8,128)S(1)} collective-permute-done((f32[176,768]{1,0:T(8,128)}, f32[176,768]{1,0:T(8,128)S(1)}, u32[]{:S(2)}, u32[]{:S(2)}) %collective-permute-start) | collective-permute-done | bytes 540704 | tf_op jit(solution)/shard_map/ppermute | solution.py:277
  41.0 0.0 copy-start
  41.0 0.8 copy-done
  41.8 2.0 %join.1.in_ref = bf16[176,768]{1,0:T(8,128)(2,1)} custom-call(f32[176,768]{1,0:T(8,128)} %get-tuple-element.7.own_ref, f32[176,768]{1,0:T(8,128)} %copy-done), custom_call_target="tpu_custom_call" | custom-call | tf_op jit(solution)/shard_map/join/pallas_call | solution.py:278
  43.8 29.8 %spread.1.kernels_ref = bf16[16,176,768]{2,1,0:T(8,128)(2,1)} custom-call(bf16[176,768]{1,0:T(8,128)(2,1)} %join.1.in_ref), custom_call_target="tpu_custom_call" | custom-call | tf_op jit(solution)/shard_map/spread/pallas_call | solution.py:286
  73.6 17.0 %apply.1 = bf16[8,16,2,16,128]{4,3,2,1,0:T(8,128)(2,1)} custom-call(bf16[16,176,768]{2,1,0:T(8,128)(2,1)} %spread.1.kernels_ref, f32[768,128]{1,0:T(8,128)} %negate_select_fusion.phase_ref, f32[176,128]{1,0:T(8,128)} %get-tuple-element.10.cos_ref, f32[176,128]{1,0:T(8,128)} %get-tuple-element.9.sin_ref, bf16[8,16,2,32,128]{4,3,2,1,0:T(8,128)(2,1)} %maps_ref.1), custom_call_target="tpu_custom_call" | custom-call | tf_op jit(solution)/shard_map/apply/pallas_call | solution.py:316
  (8 shorter events, 0.0 us)
Async XLA Ops:
  25.5 15.6 %collective-permute-start = (f32[176,768]{1,0:T(8,128)}, f32[176,768]{1,0:T(8,128)S(1)}, u32[]{:S(2)}, u32[]{:S(2)}) collective-permute-start(f32[176,768]{1,0:T(8,128)} %get-tuple-element.8), channel_id=1, source_target_pairs={{0,1},{1,0},{2,3},{3,2},{4,5},{5,4},{6,7},{7,6},{8,9},{9,8},{10,11... | collective-permute-start | bytes 1622024 | tf_op jit(solution)/shard_map/ppermute | solution.py:277
  41.0 0.8 copy-start

commit v3 on v2

--- a/solution.py
+++ b/solution.py
@@ -26,13 +26,27 @@
     )
 
 
+def store_split(ref, rows, total):
+    high = total.astype(jnp.bfloat16)
+    last = SPAN * PAIR
+    mid = CENTRE * PAIR
+    left = total[:, mid : mid + PAIR] - high[:, mid : mid + PAIR].astype(jnp.float32)
+    ref[rows, :last] = high[:, :last]
+    ref[rows, last:] = left.astype(jnp.bfloat16)
+
+
 def gram_kernel(
-    factor, share, col_ref, basis_ref, picks_ref, own_ref, other_ref, hot, order, x, xa, xb, yr, yi, tacc
+    factor, share, col_ref, basis_ref, picks_ref, own_ref, other_ref, windows_in, sems, hot, order, x, xa, xb, yr, yi, tacc
 ):
     keep, block = hot.shape
     rows = order.shape[0]
     side = KSIZE * share
     parts = COILS // share
+    loads = [
+        pltpu.make_async_copy(basis_ref.at[ri], windows_in.at[ri], sems.at[ri]) for ri in range(2)
+    ]
+    for load in loads:
+        load.start()
     lanes = lax.broadcasted_iota(jnp.int32, (keep, block), 1)
     hot[...] = (lanes == picks_ref[...]).astype(jnp.float32).astype(jnp.bfloat16)
     source = lax.broadcasted_iota(jnp.int32, (COILS, rows), 1)
@@ -48,7 +62,7 @@
     chunk = KSIZE * COILS
 
     def choose(ri, carry):
-        windows = dot_nn(hot[...], basis_ref[ri]).astype(jnp.bfloat16)
+        windows = dot_nn(hot[...], windows_in[ri]).astype(jnp.bfloat16)
 
         def permute(step, inner):
             at = pl.multiple_of(step * chunk, chunk)
@@ -59,7 +73,9 @@
 
         return lax.fori_loop(0, rows // chunk, permute, carry)
 
-    lax.fori_loop(0, 2, choose, 0)
+    for ri, load in enumerate(loads):
+        load.wait()
+        choose(ri, 0)
 
     zeros = jnp.zeros((PAIR, keep), jnp.bfloat16)
     for a in range(KSIZE):
@@ -102,17 +118,19 @@
                 at = pl.multiple_of(part * side + a * share, share)
                 term = tacc[a + p - CENTRE, pl.ds(at, share), :]
                 total = term if total is None else total + term
-            ref[p * share : (p + 1) * share, :] = total * factor
-
-
-def join_kernel(own_ref, got_ref, out_ref):
-    total = own_ref[...] + got_ref[...]
-    high = total.astype(jnp.bfloat16)
-    left = total - high.astype(jnp.float32)
+            total = total * factor
+            if part is own:
+                ref[p * share : (p + 1) * share, :] = total
+            else:
+                store_split(ref, slice(p * share, (p + 1) * share), total)
+
+
+def join_kernel(own_ref, got_ref, out_ref, total):
     last = SPAN * PAIR
-    out_ref[...] = high
     mid = CENTRE * PAIR
-    out_ref[:, last:] = left[:, mid : mid + PAIR].astype(jnp.bfloat16)
+    total[...] = own_ref[...] + got_ref[...].astype(jnp.float32)
+    total[:, mid : mid + PAIR] += got_ref[:, last:].astype(jnp.float32)
+    store_split(out_ref, slice(None), total[...])
 
 
 def spread_kernel(in_ref, out_ref, local_sem, send, got):
@@ -257,10 +275,16 @@
     part = jax.ShapeDtypeStruct((high_rows, lanes), jnp.float32)
     own, other = pl.pallas_call(
         functools.partial(gram_kernel, factor, share),
-        out_shape=(part, part),
-        in_specs=[pl.BlockSpec(memory_space=pltpu.SMEM), vmem, vmem],
+        out_shape=(part, jax.ShapeDtypeStruct((high_rows, lanes), bf16)),
+        in_specs=[
+            pl.BlockSpec(memory_space=pltpu.SMEM),
+            pl.BlockSpec(memory_space=pl.ANY),
+            vmem,
+        ],
         out_specs=(vmem, vmem),
         scratch_shapes=[
+            pltpu.VMEM((2, block, rows), bf16),
+            pltpu.SemaphoreType.DMA((2,)),
             pltpu.VMEM((keep, block), bf16),
             pltpu.VMEM((rows, rows), bf16),
             pltpu.VMEM((2, rows, keep), bf16),
@@ -280,6 +304,7 @@
         out_shape=jax.ShapeDtypeStruct((high_rows, lanes), bf16),
         in_specs=[vmem, vmem],
         out_specs=vmem,
+        scratch_shapes=[pltpu.VMEM((high_rows, lanes), jnp.float32)],
         name="join",
     )(own, got)
     n_slc = lax.axis_size("slc")

time: 91.1 us -> 84.1 us (0.923)
  waiting for transfers between devices: 7.52 us -> 1.69 us
  Pallas kernels: 72.7 us -> 71.6 us
    ppermute x1, waiting for transfers between devices: 7.52 us -> 1.69 us  [shards(): got = lax.ppermute(other, 'col', [(i, n_col - 1 - i) for i in range(n_col)])]
    pallas_call x1, Pallas kernels: 24 us -> 22.9 us  [shards(): pl.pallas_call(functools.partial(gram_kernel, factor, share), out_shape=(...]
where the time goes in v3:
time: 84.1 us; the launch traced here: 83.5 us
  Pallas kernels  71.6 us (85%)
  other arithmetic  5.02 us (6%)
  starting transfers between devices  2.99 us (4%)
  local copies, waits for them, and re-layouts  2.2 us (3%)
  waiting for transfers between devices  1.69 us (2%)
    pallas_call x1, Pallas kernels, shards(): pl.pallas_call(spread_kernel, out_shape=jax.ShapeDtypeStruct((n_slc, high...  29.8 us
    pallas_call x1, Pallas kernels, shards(): pl.pallas_call(functools.partial(gram_kernel, factor, share), out_shape=(...  22.9 us
    pallas_call x1, Pallas kernels, shards(): pl.pallas_call(functools.partial(apply_kernel, width, share), grid=(slice...  16.9 us
    select_n x1, other arithmetic, shards(): phase = jnp.where((from_imag == 1) & (to_imag == 0), -phase, phase)  3.81 us
    ppermute x1, starting transfers between devices, shards(): got = lax.ppermute(other, 'col', [(i, n_col - 1 - i) for i in range(n_col)])  2.99 us
    pallas_call x1, Pallas kernels, shards(): pl.pallas_call(join_kernel, out_shape=jax.ShapeDtypeStruct((high_rows, la...  1.93 us
    ppermute x1, waiting for transfers between devices, shards(): got = lax.ppermute(other, 'col', [(i, n_col - 1 - i) for i in range(n_col)])  1.69 us
  transfers between devices with their start and end apart: 1, of which 1 were waited for; matrix products, arithmetic and copies ran while one was open for 6% of the time, Pallas kernels for 0%

profile of v3, /device:TPU:0, one launch (start us, length us, event | category | flops | bytes accessed | tf_op | source)
XLA Modules:
  0.0 83.5 jit_solution(11099765555633371794)
XLA Ops:
  0.0 1.5 %copy.4.picks_ref = s32[304,1]{1,0:T(8,128)} copy(s32[304,1]{0,1:T(1,128)} %bitcast.6) | data formatting | bytes 2432 | tf_op jit(solution)/shard_map/reshape | solution.py:299
  1.5 22.9 %gram.1 = (f32[176,768]{1,0:T(8,128)}, bf16[176,768]{1,0:T(8,128)(2,1)}) custom-call(s32[1]{0:T(128)} %bitcast.col_ref, bf16[2,1728,1152]{2,1,0:T(8,128)(2,1)} %bitcast.5, s32[304,1]{1,0:T(8,128)} %copy.4.picks_ref), custom_call_target="tpu_custom_call" | custom-call | tf_op jit(solution)/shard_map/gram/pallas_call | solution.py:276
  24.4 3.0 %collective-permute-start = (bf16[176,768]{1,0:T(8,128)(2,1)}, bf16[176,768]{1,0:T(8,128)(2,1)S(1)}, u32[]{:S(2)}, u32[]{:S(2)}) collective-permute-start(bf16[176,768]{1,0:T(8,128)(2,1)} %get-tuple-element.8), channel_id=1, source_target_pairs={{0,1},{1,0},{2,3},{3,2},{4,5},{5,4},{6,7},{7,6},{8,9},{9,8},{10,11... | collective-permute-start | bytes 811016 | tf_op jit(solution)/shard_map/ppermute | solution.py:301
  27.4 1.2 %fusion.10 = (f32[176,128]{1,0:T(8,128)}, f32[176,128]{1,0:T(8,128)}) fusion(s32[176]{0:T(256)S(1)} %get-tuple-element.23, s32[176]{0:T(256)S(1)} %get-tuple-element.24, pred[176]{0:T(512)(128)(4,1)S(1)} %compare_and_fusion), kind=kLoop, calls=%fused_computation.26 | loop fusion | flops 360448 | bytes 181808 | tf_op jit(solution)/shard_map/sin | solution.py:358
  28.6 3.8 %negate_select_fusion.phase_ref = f32[768,128]{1,0:T(8,128)} fusion(s32[128]{0:T(128)S(1)} %get-tuple-element.19, s32[128]{0:T(128)S(1)} %get-tuple-element.21, s32[]{:T(128)S(6)} %mul.25, s32[768]{0:T(1024)S(1)} %get-tuple-element.12, s32[768]{0:T(1024)S(1)} %get-tuple-element.15, s32[128]{0:T(128)S(1)} %get-tuple-element.20, s32[128]{0:T(128)S(1)} %get-tuple-element.22, ...), kind=kLoop, calls=%fused_computation.3 | loop fusion | flops 3932160 | bytes 409348 | tf_op jit(solution)/shard_map/jit(_where)/select_n | solution.py:334
  32.4 1.7 %collective-permute-done.got_ref = bf16[176,768]{1,0:T(8,128)(2,1)S(1)} collective-permute-done((bf16[176,768]{1,0:T(8,128)(2,1)}, bf16[176,768]{1,0:T(8,128)(2,1)S(1)}, u32[]{:S(2)}, u32[]{:S(2)}) %collective-permute-start) | collective-permute-done | bytes 270368 | tf_op jit(solution)/shard_map/ppermute | solution.py:301
  34.1 0.0 copy-start
  34.1 0.7 copy-done
  34.8 1.9 %join.1.in_ref = bf16[176,768]{1,0:T(8,128)(2,1)} custom-call(f32[176,768]{1,0:T(8,128)} %get-tuple-element.7.own_ref, bf16[176,768]{1,0:T(8,128)(2,1)} %copy-done), custom_call_target="tpu_custom_call" | custom-call | tf_op jit(solution)/shard_map/join/pallas_call | solution.py:302
  36.7 29.8 %spread.1.kernels_ref = bf16[16,176,768]{2,1,0:T(8,128)(2,1)} custom-call(bf16[176,768]{1,0:T(8,128)(2,1)} %join.1.in_ref), custom_call_target="tpu_custom_call" | custom-call | tf_op jit(solution)/shard_map/spread/pallas_call | solution.py:311
  66.6 16.9 %apply.1 = bf16[8,16,2,16,128]{4,3,2,1,0:T(8,128)(2,1)} custom-call(bf16[16,176,768]{2,1,0:T(8,128)(2,1)} %spread.1.kernels_ref, f32[768,128]{1,0:T(8,128)} %negate_select_fusion.phase_ref, f32[176,128]{1,0:T(8,128)} %get-tuple-element.10.cos_ref, f32[176,128]{1,0:T(8,128)} %get-tuple-element.9.sin_ref, bf16[8,16,2,32,128]{4,3,2,1,0:T(8,128)(2,1)} %maps_ref.1), custom_call_target="tpu_custom_call" | custom-call | tf_op jit(solution)/shard_map/apply/pallas_call | solution.py:341
  (8 shorter events, 0.0 us)
Async XLA Ops:
  24.4 9.7 %collective-permute-start = (bf16[176,768]{1,0:T(8,128)(2,1)}, bf16[176,768]{1,0:T(8,128)(2,1)S(1)}, u32[]{:S(2)}, u32[]{:S(2)}) collective-permute-start(bf16[176,768]{1,0:T(8,128)(2,1)} %get-tuple-element.8), channel_id=1, source_target_pairs={{0,1},{1,0},{2,3},{3,2},{4,5},{5,4},{6,7},{7,6},{8,9},{9,8},{10,11... | collective-permute-start | bytes 811016 | tf_op jit(solution)/shard_map/ppermute | solution.py:301
  34.1 0.7 copy-start
